TPU v7x, 256 devices: a whole 4x4x8 slice. The times are simulated.
256 devices in a mesh: ctx: 16 (over z_lo, y), fsdp: 16 (over z_hi, x, core).
Axes of the slice: x: 4, y: 4, z: 8 (z_hi: 2, z_lo: 4; z = z_hi * 4 + z_lo), core: 2. Of those that a mesh axis runs over, the one named last changes fastest.
Arguments:
- inputs: bfloat16 [4096, 7168], P('ctx'), may hold values from -12 to 12
- w_qkv: bfloat16 [7168, 3, 4096], P('ctx', None, 'fsdp'), may hold values from -1 to 1, as said below
- selected: int32 [8, 4], replicated, may hold values from -1 to 7, as said below
- d_attn: bfloat16 [4096, 4096], P('ctx', 'fsdp'), may hold values from -6 to 6
Outputs:
- d_input: bfloat16 [4096, 7168], P('ctx', 'fsdp')
Inputs may be any that keep to these rules, and one draw needn't show every extreme that they name: `selected`: row b lists min(b + 1, 4) different blocks of 0 to b, b among them, in the first slots; the other slots hold -1. `w_qkv`: projection weights scaled by the fan-in.
All inputs are finite; a program needn't handle non-finite values.
Results may differ from a plain program's by a relative error of at most 0.023.
Values may be sent and summed in bfloat16 or wider, within the bound.
A program may use at most 128 MiB of HBM per device.

v0:
```python
import jax
import jax.numpy as jnp
from jax import lax
from jax.sharding import PartitionSpec as P

HD = 128
BLOCK = 512


def stat_rows(stat, row_count, heads):
    return stat[..., 0].transpose(0, 2, 1).reshape(row_count, heads)


def attend_chosen(query, keys_all, values_all, grad_out, selected, first_row):
    row_count, col_count = query.shape
    seq_len = keys_all.shape[0]
    nblocks = seq_len // BLOCK
    heads = col_count // HD
    top_count = selected.shape[1]
    group = min(BLOCK, row_count)
    groups = row_count // group
    scaling = HD ** (-0.5)
    block_ids = jnp.arange(nblocks, dtype=jnp.int32)
    q_block = (first_row + jnp.arange(groups, dtype=jnp.int32) * group) // BLOCK
    picked = q_block[:, None] == block_ids[None, :]
    chosen_ids = jnp.sum(jnp.where(picked[:, :, None], selected[None], 0), axis=1)
    index = jnp.maximum(chosen_ids, 0)
    key_pos = index[:, :, None] * BLOCK + jnp.arange(BLOCK, dtype=jnp.int32)[None, None, :]
    key_pos = key_pos.reshape(groups, top_count * BLOCK)
    slot_valid = jnp.repeat(chosen_ids >= 0, BLOCK, axis=1)
    position_q = (first_row + jnp.arange(row_count, dtype=jnp.int32)).reshape(groups, group)
    allowed = slot_valid[:, None, :] & (position_q[:, :, None] >= key_pos[:, None, :])
    key_heads = keys_all.reshape(nblocks, BLOCK, col_count)[index].reshape(
        groups, top_count * BLOCK, heads, HD
    )
    value_heads = values_all.reshape(nblocks, BLOCK, col_count)[index].reshape(
        groups, top_count * BLOCK, heads, HD
    )
    query_heads = query.reshape(groups, group, heads, HD)
    grad_heads = grad_out.reshape(groups, group, heads, HD)
    scores = (
        jnp.einsum("bqhd,bkhd->bhqk", query_heads, key_heads, preferred_element_type=jnp.float32)
        * scaling
    )
    masked = jnp.where(allowed[:, None], scores, -jnp.inf)
    highest = jnp.max(masked, axis=-1, keepdims=True)
    expo = jnp.exp(masked - highest)
    totals = jnp.sum(expo, axis=-1, keepdims=True)
    probs = expo / totals
    probs_low = probs.astype(jnp.bfloat16)
    attended = jnp.einsum(
        "bhqk,bkhd->bqhd", probs_low, value_heads, preferred_element_type=jnp.float32
    ).astype(jnp.bfloat16)
    delta_rows = jnp.sum(grad_heads.astype(jnp.float32) * attended.astype(jnp.float32), axis=3)
    delta = delta_rows.transpose(0, 2, 1)[..., None]
    dprobs = jnp.einsum(
        "bqhd,bkhd->bhqk", grad_heads, value_heads, preferred_element_type=jnp.float32
    )
    dscores = (probs * (dprobs - delta)).astype(jnp.bfloat16)
    dquery = (
        jnp.einsum("bhqk,bkhd->bqhd", dscores, key_heads, preferred_element_type=jnp.float32)
        * scaling
    )
    dquery = dquery.astype(jnp.bfloat16).reshape(row_count, col_count)
    highest_rows = stat_rows(highest, row_count, heads)
    total_rows = stat_rows(totals, row_count, heads)
    delta_flat = delta_rows.reshape(row_count, heads)
    key_slots = (
        jnp.einsum("bhqk,bqhd->bkhd", dscores, query_heads, preferred_element_type=jnp.float32)
        * scaling
    )
    value_slots = jnp.einsum(
        "bhqk,bqhd->bkhd", probs_low, grad_heads, preferred_element_type=jnp.float32
    )
    onehot = (chosen_ids[:, :, None] == block_ids[None, None, :]).astype(jnp.float32)
    key_term = jnp.einsum(
        "gtn,gtkc->nkc",
        onehot,
        key_slots.reshape(groups, top_count, BLOCK, col_count),
        precision=lax.Precision.HIGHEST,
    ).reshape(seq_len, col_count)
    value_term = jnp.einsum(
        "gtn,gtkc->nkc",
        onehot,
        value_slots.reshape(groups, top_count, BLOCK, col_count),
        precision=lax.Precision.HIGHEST,
    ).reshape(seq_len, col_count)
    return (dquery, key_term, value_term, highest_rows, total_rows, delta_flat)


def shards(inputs, w_qkv, selected, d_attn):
    row_count, width = inputs.shape
    col_count = w_qkv.shape[2]
    first_row = lax.axis_index("ctx") * row_count
    whole_w = lax.all_gather(w_qkv, "ctx", axis=0, tiled=True).reshape(width, 3 * col_count)
    projected = jnp.dot(inputs, whole_w, preferred_element_type=jnp.float32)
    projected = projected.astype(jnp.bfloat16).reshape(row_count, 3, col_count)
    query = projected[:, 0]
    keys_local = projected[:, 1]
    values_local = projected[:, 2]
    keys_all, values_all = (
        lax.all_gather(keys_local, "ctx", axis=0, tiled=True),
        lax.all_gather(values_local, "ctx", axis=0, tiled=True),
    )
    dquery, key_term, value_term, _, _, _ = attend_chosen(
        query, keys_all, values_all, d_attn, selected, first_row
    )
    key_total, value_total = (
        lax.psum_scatter(
            key_term.astype(jnp.bfloat16), "ctx", scatter_dimension=0, tiled=True
        ).astype(jnp.float32),
        lax.psum_scatter(
            value_term.astype(jnp.bfloat16), "ctx", scatter_dimension=0, tiled=True
        ).astype(jnp.float32),
    )
    key_sum = key_total.astype(jnp.bfloat16)
    value_sum = value_total.astype(jnp.bfloat16)
    flat_grads = jnp.stack([dquery, key_sum, value_sum], axis=1).reshape(row_count, 3 * col_count)
    contract = (((1,), (1,)), ((), ()))
    partial_grad = lax.dot_general(
        flat_grads, whole_w, contract, preferred_element_type=jnp.float32
    )
    total = lax.psum_scatter(
        partial_grad.astype(jnp.bfloat16), "fsdp", scatter_dimension=1, tiled=True
    )
    return total


def solution(mesh):
    placed = (P("ctx", None), P("ctx", None, "fsdp"), P(), P("ctx", "fsdp"))
    return jax.shard_map(
        shards, mesh=mesh, in_specs=placed, out_specs=P("ctx", "fsdp"), check_vma=False
    )
```

profile of v0, /device:TPU:8, one launch (start us, length us, event | category | flops | bytes accessed | tf_op | source)
XLA Modules:
  0.0 630.6 jit_solution(6221910780856533034)
XLA Ops:
  6.5 0.0 all-gather.6.cloned.1.call-start
  6.5 0.7 all-gather.6.cloned.1.call-update
  7.3 0.0 all-gather.8.cloned.1.call-start
  7.3 129.8 %all-gather.6.cloned.1.call-done = bf16[7168,3,256]{2,0,1:T(8,128)(2,1)} async-done(((bf16[448,3,256]{2,0,1:T(8,128)(2,1)}), bf16[7168,3,256]{2,0,1:T(8,128)(2,1)}) %all-gather.6.cloned.1.call-update) | async-done | bytes 11010064 | tf_op jit(solution)/shard_map/all_gather | solution.py:95
  137.1 14.8 %copy.15 = bf16[7168,3,256]{0,2,1:T(8,128)(2,1)} copy(bf16[7168,3,256]{2,0,1:T(8,128)(2,1)} %all-gather.6.cloned.1.call-done) | data formatting | bytes 22020096 | tf_op jit(solution)/shard_map/all_gather | solution.py:95
  151.9 0.0 copy-start.8
  151.9 8.3 %convolution_convert_fusion.1 = bf16[256,768]{1,0:T(8,128)(2,1)S(1)} fusion(bf16[256,7168]{1,0:T(8,128)(2,1)} %param.4, bf16[7168,768]{0,1:T(8,128)(2,1)} %bitcast.100), kind=kOutput, calls=%fused_computation.23 | convolution fusion | flops 2818768896 | bytes 15073280 | tf_op jit(solution)/shard_map/dot_general | solution.py:96
  160.2 0.2 copy.16
  160.4 0.7 fusion.39
  161.1 0.0 all-gather.8.cloned.1.call-update
  161.1 0.0 all-gather.10.cloned.1.call-start
  161.2 0.7 all-gather.10.cloned.1.call-update
  161.9 0.2 reduce-scatter.4.cloned.1.call-start
  162.2 0.0 copy-done.8
  162.2 0.1 select_reduce_fusion
  162.3 0.1 broadcast_bitcast_fusion
  162.4 0.0 copy-done.4
  162.4 0.1 copy.23
  162.5 0.1 add.48
  162.6 1.2 compare_and_fusion
  163.8 71.9 %all-gather.8.cloned.1.call-done = bf16[4096,1,256]{0,2,1:T(8,128)(2,1)} async-done(((bf16[256,1,256]{0,2,1:T(8,128)(2,1)}), bf16[4096,1,256]{0,2,1:T(8,128)(2,1)}) %all-gather.8.cloned.1.call-update) | async-done | bytes 2097168 | tf_op jit(solution)/shard_map/all_gather | solution.py:102
  235.7 3.3 copy.17
  239.0 0.6 gather_fusion
  239.6 0.3 reshape.318
  239.9 0.8 copy.26
  240.7 70.2 %all-gather.10.cloned.1.call-done = bf16[4096,1,256]{0,2,1:T(8,128)(2,1)} async-done(((bf16[256,1,256]{0,2,1:T(8,128)(2,1)}), bf16[4096,1,256]{0,2,1:T(8,128)(2,1)}) %all-gather.10.cloned.1.call-update) | async-done | bytes 2097168 | tf_op jit(solution)/shard_map/all_gather | solution.py:103
  310.9 3.3 copy.20
  314.2 1.6 gather_fusion.1
  315.8 1.4 reshape.321
  317.2 2.1 copy.24
  319.3 0.0 copy-done.5
  319.3 0.0 copy-done.6
  319.3 3.7 fusion.40
  322.9 2.9 fusion.13
  325.9 0.0 copy-done.2
  325.9 0.9 fusion.19
  326.7 0.0 copy-done.3
  326.7 0.0 copy-start.7
  326.7 0.7 fusion.2
  327.5 0.0 copy-start
  327.5 1.4 copy-done
  328.9 0.0 copy-done.7
  328.9 1.8 fusion.4
  330.7 3.6 reshape.323
  334.3 4.1 copy.27
  338.4 4.1 convolution_convert_fusion
  342.5 1.7 copy.28
  344.2 0.0 reduce-scatter.4.cloned.1.call-update
  344.3 0.3 reduce-scatter.6.cloned.1.call-start
  344.5 0.9 convolution_bitcast_fusion.1
  345.5 8.6 %copy.31 = f32[1,2048,2,128]{3,2,1,0:T(2,128)} copy(f32[1,2048,2,128]{3,1,2,0:T(8,128)S(1)} %convolution_bitcast_fusion.1) | data formatting | bytes 4194304 | tf_op jit(solution)/shard_map/bhqk,bqhd->bkhd/transpose | solution.py:72
  354.0 2.9 reshape.324
  357.0 3.4 fusion.10
  360.3 1.7 copy.33
  362.1 0.0 reduce-scatter.6.cloned.1.call-update
  362.1 0.0 reduce-scatter.8.cloned.1.call-start
  362.1 1.5 copy-done.1
  363.7 0.8 fusion.14
  364.5 0.1 copy.34
  364.6 63.0 %reduce-scatter.4.cloned.1.call-done = bf16[256,256]{1,0:T(8,128)(2,1)} async-done(((bf16[4096,256]{1,0:T(8,128)(2,1)}), bf16[256,256]{1,0:T(8,128)(2,1)}) %reduce-scatter.4.cloned.1.call-update) | async-done | bytes 131088 | tf_op jit(solution)/shard_map/reduce_scatter | solution.py:109
  427.6 86.7 %reduce-scatter.6.cloned.1.call-done = bf16[256,256]{1,0:T(8,128)(2,1)} async-done(((bf16[4096,256]{1,0:T(8,128)(2,1)}), bf16[256,256]{1,0:T(8,128)(2,1)}) %reduce-scatter.6.cloned.1.call-update) | async-done | bytes 131088 | tf_op jit(solution)/shard_map/reduce_scatter | solution.py:112
  514.2 9.3 %fusion.1 = bf16[256,7168]{0,1:T(8,128)(2,1)} fusion(bf16[7168,3,256]{2,0,1:T(8,128)(2,1)} %all-gather.6.cloned.1.call-done, bf16[256,1,256]{2,0,1:T(8,128)(2,1)} %bitcast.115, bf16[256,1,256]{2,0,1:T(8,128)(2,1)} %bitcast.114, bf16[256,1,256]{2,0,1:T(8,128)(2,1)S(1)} %copy.34), kind=kOutput, calls=%fused_computation.4 | convolution fusion | flops 2820800512 | bytes 15073280 | tf_op jit(solution)/shard_map/dot_general | solution.py:120
  523.5 0.0 reduce-scatter.8.cloned.1.call-update
  523.5 100.3 %reduce-scatter.8.cloned.1.call-done = bf16[256,448]{0,1:T(8,128)(2,1)} async-done(((bf16[256,7168]{0,1:T(8,128)(2,1)}), bf16[256,448]{0,1:T(8,128)(2,1)}) %reduce-scatter.8.cloned.1.call-update) | async-done | bytes 229392 | tf_op jit(solution)/shard_map/reduce_scatter | solution.py:123
  (15 shorter events, 0.1 us)
Async XLA Ops:
  6.5 130.5 %all-gather.6.cloned.1.call-start = ((), (), s32[]{:S(2)}) async-start(), calls=%async_computation.3 | async-start | bytes 11698176 | tf_op jit(solution)/shard_map/all_gather | solution.py:95
  7.3 228.4 %all-gather.8.cloned.1.call-start = ((), (), s32[]{:S(2)}) async-start(), calls=%async_computation.7 | async-start | bytes 2228224 | tf_op jit(solution)/shard_map/all_gather | solution.py:102
  151.9 10.3 %copy-start.8 = (s32[8,4]{0,1:T(4,128)S(1)}, s32[8,4]{0,1:T(4,128)}, u32[]{:S(2)}) copy-start(s32[8,4]{0,1:T(4,128)} %param.6) | copy-start | bytes 388
  151.9 10.5 %copy-start.4 = (bf16[256,256]{1,0:T(8,128)(2,1)S(1)}, bf16[256,256]{1,0:T(8,128)(2,1)}, u32[]{:S(2)}) copy-start(bf16[256,256]{1,0:T(8,128)(2,1)} %param.7) | copy-start | bytes 393220
  161.1 149.8 %all-gather.10.cloned.1.call-start = ((), (), s32[]{:S(2)}) async-start(), calls=%async_computation.8 | async-start | bytes 2228224 | tf_op jit(solution)/shard_map/all_gather | solution.py:103
  161.9 265.7 %reduce-scatter.4.cloned.1.call-start = ((), (), s32[]{:S(2)}) async-start(), calls=%async_computation.4 | async-start | bytes 2228224 | tf_op jit(solution)/shard_map/reduce_scatter | solution.py:109
  315.8 3.5 copy-start.5
  315.8 3.5 copy-start.6
  322.9 3.0 copy-start.2
  322.9 3.8 copy-start.3
  326.7 2.1 copy-start.7
  327.5 1.4 copy-start
  344.3 170.0 %reduce-scatter.6.cloned.1.call-start = ((), (), s32[]{:S(2)}) async-start(), calls=%async_computation.5 | async-start | bytes 2228224 | tf_op jit(solution)/shard_map/reduce_scatter | solution.py:112
  362.1 1.6 copy-start.1
  362.1 261.7 %reduce-scatter.8.cloned.1.call-start = ((), (), s32[]{:S(2)}) async-start(), calls=%async_computation.6 | async-start | bytes 3899392 | tf_op jit(solution)/shard_map/reduce_scatter | solution.py:123
Sparse Core Ops, SparseCore 0:
  9.1 127.8 all-gather.5
  161.2 74.3 all-gather.7
  237.4 73.4 all-gather.9
  344.4 83.1 reduce-scatter.3
  430.0 84.2 reduce-scatter.5
  523.6 100.1 reduce-scatter.7
where the time goes:
time: 631 us
  waiting for transfers between devices  523 us (83%)
  local copies, waits for them, and re-layouts  55 us (9%)
  matrix products  33.8 us (5%)
  between operations  13.7 us (2%)
    all_gather x1, waiting for transfers between devices, shards(): lax.all_gather(w_qkv, 'ctx', axis=0, tiled=True)  130 us
    reduce_scatter x1, waiting for transfers between devices, shards(): lax.psum_scatter(partial_grad.astype(jnp.bfloat16), 'fsdp', scatter_dimen...  100 us
    reduce_scatter x1, waiting for transfers between devices, shards(): lax.psum_scatter(value_term.astype(jnp.bfloat16), 'ctx', scatter_dimensio...  86.7 us
    all_gather x1, waiting for transfers between devices, shards(): lax.all_gather(keys_local, 'ctx', axis=0, tiled=True)  71.9 us
    all_gather x1, waiting for transfers between devices, shards(): lax.all_gather(values_local, 'ctx', axis=0, tiled=True)  70.2 us
    reduce_scatter x1, waiting for transfers between devices, shards(): lax.psum_scatter(key_term.astype(jnp.bfloat16), 'ctx', scatter_dimension=...  63 us
    another operation x7, local copies, waits for them, and re-layouts  15.3 us
    all_gather x1, local copies, waits for them, and re-layouts, shards(): lax.all_gather(w_qkv, 'ctx', axis=0, tiled=True)  14.8 us
  transfers between devices with their start and end apart: 6, of which 6 were waited for; matrix products, arithmetic and copies ran while one was open for 4% of the time, Pallas kernels for 0%

commit v1 on v0

--- a/solution.py
+++ b/solution.py
@@ -92,7 +92,9 @@
     row_count, width = inputs.shape
     col_count = w_qkv.shape[2]
     first_row = lax.axis_index("ctx") * row_count
-    whole_w = lax.all_gather(w_qkv, "ctx", axis=0, tiled=True).reshape(width, 3 * col_count)
+    whole_w = jnp.concatenate(
+        lax.all_to_all(jnp.stack([w_qkv] * lax.axis_size("ctx")), "ctx", 0, 0), axis=0
+    ).reshape(width, 3 * col_count)
     projected = jnp.dot(inputs, whole_w, preferred_element_type=jnp.float32)
     projected = projected.astype(jnp.bfloat16).reshape(row_count, 3, col_count)
     query = projected[:, 0]

time: 631 us -> 779 us (1.23)
  blocking collectives: 0 us -> 248 us
  waiting for transfers between devices: 523 us -> 392 us
  local copies, waits for them, and re-layouts: 55 us -> 84 us
    all_to_all x0 -> x1, blocking collectives: none -> 248 us  [shards(): lax.all_to_all(jnp.stack([w_qkv] * lax.axis_size('ctx')), 'ctx', 0, 0)]
    all_gather x1 -> x0, waiting for transfers between devices: 130 us -> none  [shards(): lax.all_gather(w_qkv, 'ctx', axis=0, tiled=True)]
    another operation x7 -> x9, local copies, waits for them, and re-layouts: 15.3 us -> 42.7 us  [the longest x1 20.9 us: shards(): whole_w = jnp.concatenate(lax.all_to_all(jnp.stack([w_qkv] * lax.axis_siz...]
    all_to_all x0 -> x1, local copies, waits for them, and re-layouts: none -> 16.4 us  [shards(): lax.all_to_all(jnp.stack([w_qkv] * lax.axis_size('ctx')), 'ctx', 0, 0)]
    all_gather x1 -> x0, local copies, waits for them, and re-layouts: 14.8 us -> none  [shards(): lax.all_gather(w_qkv, 'ctx', axis=0, tiled=True)]
  transfers between devices with their start and end apart: 6 -> 5, of which waited for: 6 -> 5; matrix products, arithmetic and copies ran while one was open for 4% -> 3% of each run, Pallas kernels for 0% -> 0%
where the time goes in v1:
time: 779 us; the launch traced here: 778 us
  waiting for transfers between devices  392 us (50%)
  blocking collectives  248 us (32%)
  local copies, waits for them, and re-layouts  84 us (11%)
  matrix products  34.8 us (4%)
  between operations  13.4 us (2%)
    all_to_all x1, blocking collectives, shards(): lax.all_to_all(jnp.stack([w_qkv] * lax.axis_size('ctx')), 'ctx', 0, 0)  248 us
    reduce_scatter x1, waiting for transfers between devices, shards(): lax.psum_scatter(partial_grad.astype(jnp.bfloat16), 'fsdp', scatter_dimen...  100 us
    reduce_scatter x1, waiting for transfers between devices, shards(): lax.psum_scatter(value_term.astype(jnp.bfloat16), 'ctx', scatter_dimensio...  86.3 us
    all_gather x1, waiting for transfers between devices, shards(): lax.all_gather(keys_local, 'ctx', axis=0, tiled=True)  71.4 us
    all_gather x1, waiting for transfers between devices, shards(): lax.all_gather(values_local, 'ctx', axis=0, tiled=True)  70.2 us
    reduce_scatter x1, waiting for transfers between devices, shards(): lax.psum_scatter(key_term.astype(jnp.bfloat16), 'ctx', scatter_dimension=...  63 us
    another operation x1, local copies, waits for them, and re-layouts, shards(): whole_w = jnp.concatenate(lax.all_to_all(jnp.stack([w_qkv] * lax.axis_siz...  20.9 us
    all_to_all x1, local copies, waits for them, and re-layouts, shards(): lax.all_to_all(jnp.stack([w_qkv] * lax.axis_size('ctx')), 'ctx', 0, 0)  16.4 us
  transfers between devices with their start and end apart: 5, of which 5 were waited for; matrix products, arithmetic and copies ran while one was open for 3% of the time, Pallas kernels for 0%

profile of v1, /device:TPU:8, one launch (start us, length us, event | category | flops | bytes accessed | tf_op | source)
XLA Modules:
  0.0 777.7 jit_solution(1286070850764660699)
XLA Ops:
  6.5 0.0 all-gather.5.cloned.1.call-start
  6.5 6.6 stack.8
  13.1 247.6 %all_to_all.5 = bf16[16,448,3,256]{3,1,2,0:T(8,128)(2,1)} all-to-all(bf16[16,448,3,256]{3,1,2,0:T(8,128)(2,1)} %stack.8), channel_id=1, replica_groups=mesh['ctx'=16,'fsdp'=16] {'ctx'}, dimensions={0} | all-to-all | bytes 22020096 | tf_op jit(solution)/shard_map/all_to_all | solution.py:96
  260.7 16.4 %copy.56 = bf16[16,448,3,256]{1,0,3,2:T(8,128)(2,1)} copy(bf16[16,448,3,256]{3,1,2,0:T(8,128)(2,1)} %all_to_all.5) | data formatting | bytes 22020096 | tf_op jit(solution)/shard_map/all_to_all | solution.py:96
  277.1 20.9 %reshape_reshape.3 = bf16[7168,768]{0,1:T(8,128)(2,1)} reshape(bf16[16,448,3,256]{1,0,3,2:T(8,128)(2,1)} %copy.56) | data formatting | bytes 22020096 | tf_op jit(solution)/shard_map/reshape;reshape | solution.py:97
  298.0 8.3 %convolution_convert_fusion.2 = bf16[256,768]{1,0:T(8,128)(2,1)S(1)} fusion(bf16[256,7168]{1,0:T(8,128)(2,1)} %param.4, bf16[7168,768]{0,1:T(8,128)(2,1)} %reshape_reshape.3), kind=kOutput, calls=%fused_computation.22 | convolution fusion | flops 2818768896 | bytes 15073280 | tf_op jit(solution)/shard_map/dot_general | solution.py:98
  306.3 0.2 copy.57
  306.5 0.7 fusion.32
  307.2 0.0 all-gather.5.cloned.1.call-update
  307.2 0.0 all-gather.7.cloned.1.call-start
  307.3 0.7 all-gather.7.cloned.1.call-update
  308.0 0.2 reduce-scatter.4.cloned.1.call-start
  308.3 0.0 copy-done.8
  308.3 0.1 select_reduce_fusion
  308.4 0.1 broadcast_bitcast_fusion
  308.5 0.0 copy-done.4
  308.5 0.1 copy.64
  308.6 0.1 add.48
  308.7 1.2 compare_and_fusion
  309.9 71.4 %all-gather.5.cloned.1.call-done = bf16[4096,1,256]{0,2,1:T(8,128)(2,1)} async-done(((bf16[256,1,256]{0,2,1:T(8,128)(2,1)}), bf16[4096,1,256]{0,2,1:T(8,128)(2,1)}) %all-gather.5.cloned.1.call-update) | async-done | bytes 2097168 | tf_op jit(solution)/shard_map/all_gather | solution.py:104
  381.4 3.3 copy.58
  384.6 0.6 gather_fusion
  385.3 0.3 reshape.318
  385.6 0.8 copy.67
  386.4 70.2 %all-gather.7.cloned.1.call-done = bf16[4096,1,256]{0,2,1:T(8,128)(2,1)} async-done(((bf16[256,1,256]{0,2,1:T(8,128)(2,1)}), bf16[4096,1,256]{0,2,1:T(8,128)(2,1)}) %all-gather.7.cloned.1.call-update) | async-done | bytes 2097168 | tf_op jit(solution)/shard_map/all_gather | solution.py:105
  456.6 3.3 copy.61
  459.9 1.6 gather_fusion.1
  461.5 1.4 reshape.321
  462.9 2.1 copy.65
  464.9 0.0 copy-done.5
  464.9 0.0 copy-done.6
  464.9 3.5 fusion.33
  468.5 2.9 fusion.12
  471.4 0.0 copy-done.2
  471.4 0.8 fusion.18
  472.3 0.0 copy-done.3
  472.3 0.0 copy-start.7
  472.3 0.7 fusion.1
  473.0 1.3 copy-done
  474.4 0.0 copy-done.7
  474.4 1.8 fusion.3
  476.2 3.6 reshape.323
  479.8 4.1 copy.68
  483.9 4.1 convolution_convert_fusion.1
  488.0 1.7 copy.69
  489.7 0.0 reduce-scatter.4.cloned.1.call-update
  489.8 0.3 reduce-scatter.6.cloned.1.call-start
  490.0 0.9 convolution_bitcast_fusion
  491.0 8.6 %copy.72 = f32[1,2048,2,128]{3,2,1,0:T(2,128)} copy(f32[1,2048,2,128]{3,1,2,0:T(8,128)S(1)} %convolution_bitcast_fusion) | data formatting | bytes 4194304 | tf_op jit(solution)/shard_map/bhqk,bqhd->bkhd/transpose | solution.py:72
  499.6 2.9 reshape.324
  502.5 3.4 fusion.9
  505.9 1.7 copy.74
  507.6 0.0 reduce-scatter.6.cloned.1.call-update
  507.6 0.3 reduce-scatter.8.cloned.1.call-start
  507.9 1.3 copy-done.1
  509.2 0.8 fusion.13
  510.0 0.1 copy.75
  510.1 63.0 %reduce-scatter.4.cloned.1.call-done = bf16[256,256]{1,0:T(8,128)(2,1)} async-done(((bf16[4096,256]{1,0:T(8,128)(2,1)}), bf16[256,256]{1,0:T(8,128)(2,1)}) %reduce-scatter.4.cloned.1.call-update) | async-done | bytes 131088 | tf_op jit(solution)/shard_map/reduce_scatter | solution.py:111
  573.1 86.3 %reduce-scatter.6.cloned.1.call-done = bf16[256,256]{1,0:T(8,128)(2,1)} async-done(((bf16[4096,256]{1,0:T(8,128)(2,1)}), bf16[256,256]{1,0:T(8,128)(2,1)}) %reduce-scatter.6.cloned.1.call-update) | async-done | bytes 131088 | tf_op jit(solution)/shard_map/reduce_scatter | solution.py:114
  659.5 1.0 pad_maximum_fusion
  660.5 0.2 copy.76
  660.7 10.4 %convolution_convert_fusion = bf16[256,7168]{0,1:T(8,128)(2,1)} fusion(bf16[256,768]{0,1:T(8,128)(2,1)S(1)} %bitcast.110, bf16[7168,768]{0,1:T(8,128)(2,1)} %reshape_reshape.3), kind=kOutput, calls=%fused_computation.3 | convolution fusion | flops 2820407296 | bytes 15073280 | tf_op jit(solution)/shard_map/dot_general | solution.py:122
  671.0 0.0 reduce-scatter.8.cloned.1.call-update
  671.1 100.1 %reduce-scatter.8.cloned.1.call-done = bf16[256,448]{0,1:T(8,128)(2,1)} async-done(((bf16[256,7168]{0,1:T(8,128)(2,1)}), bf16[256,448]{0,1:T(8,128)(2,1)}) %reduce-scatter.8.cloned.1.call-update) | async-done | bytes 229392 | tf_op jit(solution)/shard_map/reduce_scatter | solution.py:125
  (17 shorter events, 0.1 us)
Async XLA Ops:
  6.5 374.8 %all-gather.5.cloned.1.call-start = ((), (), s32[]{:S(2)}) async-start(), calls=%async_computation.7 | async-start | bytes 2228224 | tf_op jit(solution)/shard_map/all_gather | solution.py:104
  298.0 10.3 %copy-start.8 = (s32[8,4]{0,1:T(4,128)S(1)}, s32[8,4]{0,1:T(4,128)}, u32[]{:S(2)}) copy-start(s32[8,4]{0,1:T(4,128)} %param.6) | copy-start | bytes 388
  298.0 10.5 %copy-start.4 = (bf16[256,256]{1,0:T(8,128)(2,1)S(1)}, bf16[256,256]{1,0:T(8,128)(2,1)}, u32[]{:S(2)}) copy-start(bf16[256,256]{1,0:T(8,128)(2,1)} %param.7) | copy-start | bytes 393220
  307.2 149.4 %all-gather.7.cloned.1.call-start = ((), (), s32[]{:S(2)}) async-start(), calls=%async_computation.8 | async-start | bytes 2228224 | tf_op jit(solution)/shard_map/all_gather | solution.py:105
  308.0 265.1 %reduce-scatter.4.cloned.1.call-start = ((), (), s32[]{:S(2)}) async-start(), calls=%async_computation.4 | async-start | bytes 2228224 | tf_op jit(solution)/shard_map/reduce_scatter | solution.py:111
  461.4 3.5 copy-start.5
  461.5 3.5 copy-start.6
  468.5 3.0 copy-start.2
  468.5 3.8 copy-start.3
  472.3 2.1 copy-start.7
  473.0 1.4 copy-start
  489.8 169.7 %reduce-scatter.6.cloned.1.call-start = ((), (), s32[]{:S(2)}) async-start(), calls=%async_computation.5 | async-start | bytes 2228224 | tf_op jit(solution)/shard_map/reduce_scatter | solution.py:114
  507.6 1.6 copy-start.1
  507.6 263.5 %reduce-scatter.8.cloned.1.call-start = ((), (), s32[]{:S(2)}) async-start(), calls=%async_computation.6 | async-start | bytes 3899392 | tf_op jit(solution)/shard_map/reduce_scatter | solution.py:125
Sparse Core Ops, SparseCore 0:
  307.4 73.9 all-gather.4
  383.1 73.4 all-gather.6
  489.9 83.1 reduce-scatter.3
  575.5 83.9 reduce-scatter.5
  671.2 99.9 reduce-scatter.7
